TPU v7x, 256 devices: a whole 4x4x8 slice. The times are simulated.
256 devices in a mesh: frame: 64 (over z, x, core), chan: 4 (over y).
Axes of the slice: x: 4, y: 4, z: 8, core: 2. Of those that a mesh axis runs over, the one named last changes fastest.
Arguments:
- query_act: bfloat16 [56320, 2240], P('frame', 'chan'), may hold values from -6 to 6
- key_act: bfloat16 [56320, 2240], P('frame', 'chan'), may hold values from -6 to 6
- value_act: bfloat16 [56320, 2240], P('frame', 'chan'), may hold values from -6 to 6
- conv_weight: bfloat16 [3, 2240, 2240], P(None, 'chan'), may hold values from -0.109375 to 0.109375
- gate_act: bfloat16 [56320, 2240], P('frame', 'chan'), may hold values from -8 to 8
Outputs:
- layer_out: bfloat16 [56320, 2240], P('frame', 'chan')
All inputs are finite; a program needn't handle non-finite values.
Results may differ from a plain program's by a relative error of at most 0.015.
Values may be sent and summed in bfloat16 or wider, within the bound.
No kernel may reach another device: no remote copies, remote signals or barrier semaphores. Data moves between devices by JAX's collectives and lax.ppermute only.
A program may use at most 128 MiB of HBM per device.

v0:
```python
import jax
import jax.numpy as jnp
from jax import lax
from jax.sharding import PartitionSpec as P

HD = 112
TPF = 880


def padded(shard, sides, width):
    for axis, dim in sides:
        count, length = (lax.axis_size(axis), shard.shape[dim])
        up = [(i, (i + 1) % count) for i in range(count - 1)]
        down = [(j, i) for i, j in up]
        last = lax.slice_in_dim(shard, length - width, length, axis=dim)
        initial = lax.slice_in_dim(shard, 0, width, axis=dim)
        before = lax.ppermute(last, axis, up)
        after = lax.ppermute(initial, axis, down)
        shard = jnp.concatenate([before, shard, after], axis=dim)
    return shard


def shards(query_act, key_act, value_act, conv_weight, gate_act):
    row_count, chan_width = query_act.shape
    head_count = chan_width // HD
    frame_count = row_count // TPF
    key_feat = jnp.maximum(key_act, 0).reshape(frame_count, TPF, head_count, HD)
    value_feat = value_act.reshape(frame_count, TPF, head_count, HD)
    query_feat = jnp.maximum(query_act, 0).reshape(frame_count, TPF, head_count, HD)
    frame_state = jnp.einsum(
        "ftha,fthb->fhab", key_feat, value_feat, preferred_element_type=jnp.float32
    )
    local_prefix = jnp.cumsum(frame_state, axis=0)
    own_total = local_prefix[frame_count - 1]
    my_index = lax.axis_index("frame")
    state_shape = own_total.shape
    pieces = lax.all_gather(
        own_total[None].astype(jnp.bfloat16), "frame", axis=0, tiled=True
    ).astype(jnp.float32)
    piece_count = pieces.shape[0]
    source_ids = jnp.arange(piece_count, dtype=jnp.int32)
    lower_mask = (source_ids < my_index).astype(jnp.float32)
    flat_pieces = pieces.reshape(piece_count, -1)
    summed = jnp.dot(
        lower_mask[None, :],
        flat_pieces,
        precision=lax.Precision.HIGHEST,
        preferred_element_type=jnp.float32,
    )
    earlier = summed.reshape(state_shape)
    prefix_state = (local_prefix + earlier[None]).astype(jnp.bfloat16)
    readout = jnp.einsum(
        "ftha,fhab->fthb", query_feat, prefix_state, preferred_element_type=jnp.float32
    )
    scale_inv = lax.rsqrt(jnp.mean(readout * readout, axis=-1, keepdims=True) + 1e-06)
    attended = (readout * scale_inv).astype(jnp.bfloat16).reshape(row_count, chan_width)
    with_rims = padded(attended, (("frame", 0),), TPF)
    partials = jnp.dot(with_rims[0:row_count], conv_weight[0], preferred_element_type=jnp.float32)
    partials = partials + jnp.dot(
        with_rims[TPF : TPF + row_count], conv_weight[1], preferred_element_type=jnp.float32
    )
    partials = partials + jnp.dot(
        with_rims[2 * TPF : 2 * TPF + row_count], conv_weight[2], preferred_element_type=jnp.float32
    )
    conv_out = lax.psum_scatter(
        partials.astype(jnp.bfloat16), "chan", scatter_dimension=1, tiled=True
    ).astype(jnp.float32)
    gate_value = jax.nn.silu(gate_act.astype(jnp.float32))
    return (conv_out * gate_value).astype(jnp.bfloat16)


def solution(mesh):
    return jax.shard_map(
        shards,
        mesh=mesh,
        in_specs=(
            P("frame", "chan"),
            P("frame", "chan"),
            P("frame", "chan"),
            P(None, "chan", None),
            P("frame", "chan"),
        ),
        out_specs=P("frame", "chan"),
        check_vma=False,
    )
```

profile of v0, /device:TPU:1, one launch (start us, length us, event | category | flops | bytes accessed | tf_op | source)
XLA Modules:
  0.0 225.9 jit_solution(8663559478288618343)
XLA Ops:
  6.5 0.0 copy-start
  6.5 0.0 all-gather.3.cloned.1.call-start
  6.5 1.4 broadcast_maximum_fusion.1
  7.9 0.1 copy-done
  8.0 1.1 fusion.25
  9.2 0.0 all-gather.3.cloned.1.call-update
  9.2 0.0 reduce-scatter.2.cloned.1.call-start
  9.2 1.3 broadcast_maximum_fusion
  10.5 87.6 %all-gather.3.cloned.1.call-done = bf16[320,112,112]{2,1,0:T(8,128)(2,1)} async-done(((bf16[5,112,112]{2,1,0:T(8,128)(2,1)}), bf16[320,112,112]{2,1,0:T(8,128)(2,1)}) %all-gather.3.cloned.1.call-update) | async-done | bytes 8028176 | tf_op jit(solution)/shard_map/all_gather | solution.py:37
  98.2 14.1 %reshape.49 = bf16[64,62720]{1,0:T(8,128)(2,1)} reshape(bf16[320,112,112]{2,1,0:T(8,128)(2,1)} %all-gather.3.cloned.1.call-done) | data formatting | bytes 16056320 | tf_op jit(solution)/shard_map/reshape | solution.py:43
  112.3 20.4 %dot_general.26 = bf16[5,112,112,64]{2,1,0,3:T(8,128)(2,1)} reshape(bf16[62720,64]{0,1:T(8,128)(2,1)} %bitcast.41) | data formatting | bytes 16056320 | tf_op jit(solution)/shard_map/dot_general | solution.py:44
  132.6 5.1 %fusion = f32[1,5,112,112]{3,0,2,1:T(1,128)S(1)} fusion(bf16[5,112,112,64]{2,1,0,3:T(8,128)(2,1)} %dot_general.26, s32[]{:T(128)S(6)} %axis_index.15), kind=kOutput, calls=%fused_computation | convolution fusion | flops 8028224 | bytes 8279044 | tf_op jit(solution)/shard_map/dot_general | solution.py:44
  137.7 0.5 fusion.17
  138.2 0.1 fusion.18
  138.4 0.0 slice-start
  138.4 0.0 slice-start.1
  138.4 2.4 %collective-permute-start = (bf16[880,560]{0,1:T(8,128)(2,1)S(1)}, bf16[880,560]{0,1:T(8,128)(2,1)S(1)}, u32[]{:S(2)}, u32[]{:S(2)}) collective-permute-start(bf16[880,560]{0,1:T(8,128)(2,1)S(1)} %bitcast.45), channel_id=1, source_target_pairs={{0,4},{4,8},{8,12},{12,16},{16,20},{20,24},{24,28},{28,32},{32,36}... | collective-permute-start | bytes 2956808 | tf_op jit(solution)/shard_map/ppermute | solution.py:17
  140.8 2.6 %collective-permute-start.1 = (bf16[880,560]{0,1:T(8,128)(2,1)S(1)}, bf16[880,560]{0,1:T(8,128)(2,1)S(1)}, u32[]{:S(2)}, u32[]{:S(2)}) collective-permute-start(bf16[880,560]{0,1:T(8,128)(2,1)S(1)} %bitcast.46), channel_id=1, source_target_pairs={{4,0},{8,4},{12,8},{16,12},{20,16},{24,20},{28,24},{32,28},{36,32}... | collective-permute-start | bytes 2956808 | tf_op jit(solution)/shard_map/ppermute | solution.py:18
  143.4 7.6 %fusion.6 = f32[880,2240]{0,1:T(8,128)} fusion(bf16[880,560]{0,1:T(8,128)(2,1)S(1)} %bitcast.47, bf16[3,560,2240]{2,1,0:T(8,128)(2,1)} %param.8), kind=kOutput, calls=%fused_computation.5 | convolution fusion | flops 2207744000 | bytes 11450880 | tf_op jit(solution)/shard_map/dot_general | solution.py:59
  150.9 1.1 collective-permute-done
  152.0 0.0 slice-done
  152.0 0.0 slice-done.1
  152.0 5.9 %fusion.8 = f32[880,2240]{0,1:T(8,128)} fusion(bf16[880,560]{0,1:T(8,128)(2,1)S(1)} %collective-permute-done, bf16[3,560,2240]{2,1,0:T(8,128)(2,1)S(1)} %bitcast.49), kind=kOutput, calls=%fused_computation.7 | convolution fusion | flops 2207744000 | bytes 11468800 | tf_op jit(solution)/shard_map/dot_general | solution.py:58
  157.9 0.0 copy-start.2
  157.9 0.0 collective-permute-done.1
  157.9 0.0 copy-start.1
  157.9 9.1 %add_convert_fusion = bf16[880,2240]{0,1:T(8,128)(2,1)} fusion(f32[880,2240]{0,1:T(8,128)} %fusion.8, f32[880,2240]{0,1:T(8,128)} %fusion.6, bf16[880,560]{0,1:T(8,128)(2,1)S(1)} %collective-permute-done.1, bf16[3,560,2240]{2,1,0:T(8,128)(2,1)S(1)} %bitcast.49), kind=kOutput, calls=%fused_computation.2 | convolution fusion | flops 2213657600 | bytes 23296000 | tf_op jit(solution)/shard_map/dot_general | solution.py:62
  167.0 0.0 reduce-scatter.2.cloned.1.call-update
  167.0 49.2 %reduce-scatter.2.cloned.1.call-done = bf16[880,560]{0,1:T(8,128)(2,1)} async-done(((bf16[880,2240]{0,1:T(8,128)(2,1)}), bf16[880,560]{0,1:T(8,128)(2,1)}) %reduce-scatter.2.cloned.1.call-update) | async-done | bytes 985616 | tf_op jit(solution)/shard_map/reduce_scatter | solution.py:65
  216.2 0.0 copy-done.2
  216.2 2.8 %fusion.19 = bf16[880,560]{0,1:T(8,128)(2,1)} fusion(bf16[880,560]{0,1:T(8,128)(2,1)S(1)} %copy-done.2, bf16[880,560]{0,1:T(8,128)(2,1)} %reduce-scatter.2.cloned.1.call-done), kind=kLoop, calls=%fused_computation.22 | loop fusion | flops 3942400 | bytes 2956800 | tf_op jit(solution)/shard_map/convert_element_type | solution.py:69
  219.0 0.0 copy-done.1
  (2 shorter events, 0.0 us)
Async XLA Ops:
  6.5 1.5 copy-start
  6.5 91.6 %all-gather.3.cloned.1.call-start = ((), (), s32[]{:S(2)}) async-start(), calls=%async_computation.2 | async-start | bytes 9318400 | tf_op jit(solution)/shard_map/all_gather | solution.py:37
  9.2 207.0 %reduce-scatter.2.cloned.1.call-start = ((), (), s32[]{:S(2)}) async-start(), calls=%async_computation.1 | async-start | bytes 5017600 | tf_op jit(solution)/shard_map/reduce_scatter | solution.py:65
  138.4 13.7 %slice-start = ((s8[7741440]{0:T(1024)(128)(4,1)}), s8[4194304]{0:T(1024)(128)(4,1)S(1)}, s32[]{:S(2)}) async-start(s8[7741440]{0:T(1024)(128)(4,1)} %bitcast.48), calls=%async_computation.3 | async-start | bytes 8388608
  138.4 13.7 %slice-start.1 = ((s8[7741440]{0:T(1024)(128)(4,1)}), s8[3547136]{0:T(1024)(128)(4,1)S(1)}, s32[]{:S(2)}) async-start(s8[7741440]{0:T(1024)(128)(4,1)} %bitcast.48), calls=%async_computation.4 | async-start | bytes 7094272
  138.4 13.6 %collective-permute-start = (bf16[880,560]{0,1:T(8,128)(2,1)S(1)}, bf16[880,560]{0,1:T(8,128)(2,1)S(1)}, u32[]{:S(2)}, u32[]{:S(2)}) collective-permute-start(bf16[880,560]{0,1:T(8,128)(2,1)S(1)} %bitcast.45), channel_id=1, source_target_pairs={{0,4},{4,8},{8,12},{12,16},{16,20},{20,24},{24,28},{28,32},{32,36}... | collective-permute-start | bytes 2956808 | tf_op jit(solution)/shard_map/ppermute | solution.py:17
  140.8 17.1 %collective-permute-start.1 = (bf16[880,560]{0,1:T(8,128)(2,1)S(1)}, bf16[880,560]{0,1:T(8,128)(2,1)S(1)}, u32[]{:S(2)}, u32[]{:S(2)}) collective-permute-start(bf16[880,560]{0,1:T(8,128)(2,1)S(1)} %bitcast.46), channel_id=1, source_target_pairs={{4,0},{8,4},{12,8},{16,12},{20,16},{24,20},{28,24},{32,28},{36,32}... | collective-permute-start | bytes 2956808 | tf_op jit(solution)/shard_map/ppermute | solution.py:18
  157.9 58.3 %copy-start.2 = (bf16[880,560]{0,1:T(8,128)(2,1)S(1)}, bf16[880,560]{0,1:T(8,128)(2,1)}, u32[]{:S(2)}) copy-start(bf16[880,560]{0,1:T(8,128)(2,1)} %param.9) | copy-start | bytes 2956804
  157.9 61.1 %copy-start.1 = (bf16[880,560]{0,1:T(8,128)(2,1)S(1)}, bf16[880,560]{0,1:T(8,128)(2,1)}, u32[]{:S(2)}) copy-start(bf16[880,560]{0,1:T(8,128)(2,1)} %param.7) | copy-start | bytes 2956804
Sparse Core Ops, SparseCore 0:
  10.0 88.1 all-gather.2
  167.1 49.0 reduce-scatter.1
where the time goes:
time: 226 us
  waiting for transfers between devices  138 us (61%)
  local copies, waits for them, and re-layouts  34.6 us (15%)
  matrix products  29.2 us (13%)
  between operations  13.5 us (6%)
  other arithmetic  5.62 us (2%)
  starting transfers between devices  5.01 us (2%)
    all_gather x1, waiting for transfers between devices, shards(): lax.all_gather(own_total[None].astype(jnp.bfloat16), 'frame', axis=0, til...  87.6 us
    reduce_scatter x1, waiting for transfers between devices, shards(): lax.psum_scatter(partials.astype(jnp.bfloat16), 'chan', scatter_dimension...  49.2 us
    dot_general x1, local copies, waits for them, and re-layouts, shards(): jnp.dot(lower_mask[None, :], flat_pieces, precision=lax.Precision.HIGHEST...  20.4 us
    reshape x1, local copies, waits for them, and re-layouts, shards(): flat_pieces = pieces.reshape(piece_count, -1)  14.1 us
    dot_general x1, matrix products, shards(): jnp.dot(with_rims[2 * TPF:2 * TPF + row_count], conv_weight[2], preferred...  9.08 us
    dot_general x1, matrix products, shards(): jnp.dot(with_rims[TPF:TPF + row_count], conv_weight[1], preferred_element...  7.58 us
    dot_general x1, matrix products, shards(): jnp.dot(with_rims[0:row_count], conv_weight[0], preferred_element_type=jn...  5.87 us
    dot_general x1, matrix products, shards(): jnp.dot(lower_mask[None, :], flat_pieces, precision=lax.Precision.HIGHEST...  5.07 us
  transfers between devices with their start and end apart: 4, of which 3 were waited for; matrix products, arithmetic and copies ran while one was open for 7% of the time, Pallas kernels for 0%

commit v1 on v0

v1 whole, which is shorter than its diff:
```python
import jax
import jax.numpy as jnp
from jax import lax
from jax.sharding import Mesh, PartitionSpec as P

HD = 112
TPF = 880
BF = jnp.bfloat16
F32 = jnp.float32
NZ, NX, NC, NY = 8, 4, 2, 4
FR = ("z", "x", "c")


def shift(value, axis, step):
    count = lax.axis_size(axis)
    return lax.ppermute(value, axis, [(i, i + step) for i in range(count) if 0 <= i + step < count])


def ring(value, axis, step):
    count = lax.axis_size(axis)
    return lax.ppermute(value, axis, [(i, (i + step) % count) for i in range(count)])


def earlier_frames(state):
    half = state.shape[0] // 2
    core = lax.axis_index("c")
    x_at = lax.axis_index("x")
    mine = lax.dynamic_slice_in_dim(state, core * half, half, 0)
    other = lax.dynamic_slice_in_dim(state, (1 - core) * half, half, 0)
    theirs = lax.ppermute(other.astype(BF), "c", [(0, 1), (1, 0)]).astype(F32)
    chip = mine + theirs
    chip_bf = chip.astype(BF)
    total, before = chip, jnp.zeros_like(chip)
    for step in (1, 2, 3):
        got = ring(chip_bf, "x", step).astype(F32)
        total = total + got
        before = before + jnp.where(x_at >= step, got, 0.0)
    total_bf = total.astype(BF)
    one = shift(total_bf, "z", 1).astype(F32)
    two = shift(total_bf, "z", 2).astype(F32)
    near = one + two
    window = (total + near).astype(BF)
    three = shift(window, "z", 3).astype(F32)
    six = shift(window, "z", 6).astype(F32)
    before = before + (near + (three + six))
    to_other = jnp.where(core == 0, before + mine, before)
    to_self = jnp.where(core == 0, before, before + theirs)
    from_other = lax.ppermute(to_other.astype(BF), "c", [(0, 1), (1, 0)]).astype(F32)
    first = jnp.where(core == 0, to_self, from_other)
    second = jnp.where(core == 0, from_other, to_self)
    return jnp.concatenate([first, second], axis=0)


def attend(query, prefix):
    readout = jnp.einsum("hab,hat->hbt", prefix, jnp.maximum(query, 0), preferred_element_type=F32)
    scale = lax.rsqrt(jnp.mean(readout * readout, axis=1, keepdims=True) + 1e-06)
    return (readout * scale).astype(BF).reshape(-1, query.shape[-1])


def shards(query_act, key_act, value_act, conv_weight, gate_act):
    heads = query_act.shape[1] // HD
    width = heads * HD
    turned = lambda a: a.T.reshape(heads, HD, TPF)
    query = turned(query_act)
    q_prev = shift(query, FR, 1)
    q_next = shift(query, FR, -1)
    key = jnp.maximum(turned(key_act), 0)
    state = jnp.einsum("hat,hbt->hab", key, turned(value_act), preferred_element_type=F32)
    s_next = shift(state.astype(BF), FR, -1).astype(F32)
    earlier = earlier_frames(state.reshape(width, HD)).reshape(state.shape)
    me = lax.axis_index("y")
    flat = conv_weight.reshape(3 * width, NY * width)
    taps = []
    for away in range(NY):
        piece = lax.dynamic_slice_in_dim(flat, ((me + away) % NY) * width, width, 1)
        taps.append(lax.optimization_barrier(piece.T))
    here = earlier + state
    att = jnp.concatenate(
        [
            attend(q_prev, earlier.astype(BF)),
            attend(query, here.astype(BF)),
            attend(q_next, (here + s_next).astype(BF)),
        ],
        axis=0,
    )
    part = lambda away: jnp.dot(taps[away], att, preferred_element_type=F32)
    cut = (width // 2 + 15) // 16 * 16
    far = part(2).astype(BF)
    a_up = ring(far[:cut], "y", 1)
    a_down = ring(far[cut:], "y", -1)
    up = part(1)
    down = part(3)
    b_up = ring(up[cut:].astype(BF), "y", 1)
    b_down = ring(down[:cut].astype(BF), "y", -1)
    own = part(0)
    c_up = ring((up[:cut] + a_up.astype(F32)).astype(BF), "y", 1)
    c_down = ring((down[cut:] + a_down.astype(F32)).astype(BF), "y", -1)
    top = own[:cut] + c_up.astype(F32) + b_down.astype(F32)
    bottom = own[cut:] + b_up.astype(F32) + c_down.astype(F32)
    gate = jax.nn.silu(gate_act.T.astype(F32))
    out = jnp.concatenate([(top * gate[:cut]).astype(BF), (bottom * gate[cut:]).astype(BF)], axis=0)
    return out.T


def solution(mesh):
    fine = Mesh(mesh.devices.reshape(NZ, NX, NC, NY), FR + ("y",))
    act = P(FR, "y")
    return jax.shard_map(
        shards,
        mesh=fine,
        in_specs=(act, act, act, P(None, "y", None), act),
        out_specs=act,
        check_vma=False,
    )
```

time: 226 us -> 108 us (0.48)
  waiting for transfers between devices: 138 us -> 27.5 us
  starting transfers between devices: 5.01 us -> 42.1 us
  local copies, waits for them, and re-layouts: 34.6 us -> 14.4 us
  matrix products: 29.2 us -> 15.5 us
  between operations: 13.5 us -> 0.38 us
    all_gather x1 -> x0, waiting for transfers between devices: 87.6 us -> none  [shards(): lax.all_gather(own_total[None].astype(jnp.bfloat16), 'frame', axis=0, til...]
    reduce_scatter x1 -> x0, waiting for transfers between devices: 49.2 us -> none  [shards(): lax.psum_scatter(partials.astype(jnp.bfloat16), 'chan', scatter_dimension...]
    ppermute x2 -> x18, starting transfers between devices: 4.96 us -> 42.1 us  [the longest x7 27.5 us: shift(): lax.ppermute(value, axis, [(i, i + step) for i in range(count) if 0 <= i...]
    ppermute x2 -> x18, waiting for transfers between devices: 1.08 us -> 27.5 us  [the longest x9 26.6 us: ring(): lax.ppermute(value, axis, [(i, (i + step) % count) for i in range(count)])]
    dot_general x1 -> x0, local copies, waits for them, and re-layouts: 20.4 us -> none  [shards(): jnp.dot(lower_mask[None, :], flat_pieces, precision=lax.Precision.HIGHEST...]
    reshape x1 -> x0, local copies, waits for them, and re-layouts: 14.1 us -> none  [shards(): flat_pieces = pieces.reshape(piece_count, -1)]
    dot_general x6 -> x8, matrix products: 29.2 us -> 15.5 us  [the longest x4 9.14 us: shards(): part = lambda away: jnp.dot(taps[away], att, preferred_element_type=F32)]
    transpose x0 -> x1, local copies, waits for them, and re-layouts: none -> 12.1 us  [shards(): taps.append(lax.optimization_barrier(piece.T))]
  transfers between devices with their start and end apart: 4 -> 18, of which waited for: 3 -> 8; matrix products, arithmetic and copies ran while one was open for 7% -> 23% of each run, Pallas kernels for 0% -> 0%
where the time goes in v1:
time: 108 us; the launch traced here: 107 us
  starting transfers between devices  42.1 us (39%)
  waiting for transfers between devices  27.5 us (25%)
  matrix products  15.5 us (14%)
  local copies, waits for them, and re-layouts  14.4 us (13%)
  other arithmetic  7.34 us (7%)
    ppermute x7, starting transfers between devices, shift(): lax.ppermute(value, axis, [(i, i + step) for i in range(count) if 0 <= i...  27.5 us
    ppermute x9, waiting for transfers between devices, ring(): lax.ppermute(value, axis, [(i, (i + step) % count) for i in range(count)])  26.6 us
    transpose x1, local copies, waits for them, and re-layouts, shards(): taps.append(lax.optimization_barrier(piece.T))  12.1 us
    ppermute x9, starting transfers between devices, ring(): lax.ppermute(value, axis, [(i, (i + step) % count) for i in range(count)])  10.7 us
    dot_general x4, matrix products, shards(): part = lambda away: jnp.dot(taps[away], att, preferred_element_type=F32)  9.14 us
    dot_general x3, matrix products, attend(): jnp.einsum('hab,hat->hbt', prefix, jnp.maximum(query, 0), preferred_eleme...  5.21 us
    ppermute x1, starting transfers between devices, earlier_frames(): theirs = lax.ppermute(other.astype(BF), 'c', [(0, 1), (1, 0)]).astype(F32)  3.29 us
  transfers between devices with their start and end apart: 18, of which 8 were waited for; matrix products, arithmetic and copies ran while one was open for 23% of the time, Pallas kernels for 0%

profile of v1, /device:TPU:1, one launch (start us, length us, event | category | flops | bytes accessed | tf_op | source)
XLA Modules:
  0.0 107.2 jit_solution(12196274536144374920)
XLA Ops:
  0.0 1.4 %broadcast_maximum_fusion = bf16[880,560]{0,1:T(8,128)(2,1)S(1)} fusion(bf16[880,560]{0,1:T(8,128)(2,1)} %param.6), kind=kLoop, calls=%fused_computation.41 | loop fusion | flops 492800 | bytes 1971200 | tf_op jit(solution)/shard_map/max | solution.py:67
  1.4 0.1 copy-done
  1.5 1.1 %fusion.35 = (bf16[5,112,112]{2,1,0:T(8,128)(2,1)}, f32[5,112,112]{2,1,0:T(8,128)S(1)}) fusion(bf16[5,112,880]{2,1,0:T(8,128)(2,1)S(1)} %bitcast.51, bf16[5,112,880]{2,1,0:T(8,128)(2,1)S(1)} %bitcast.42), kind=kOutput, calls=%fused_computation.77 | convolution fusion | flops 110449920 | bytes 2347520 | tf_op jit(solution)/shard_map/hat,hbt->hab/dot_general | solution.py:68
  2.7 3.3 %collective-permute-start = (bf16[280,112]{1,0:T(8,128)(2,1)S(1)}, bf16[280,112]{1,0:T(8,128)(2,1)S(1)}, u32[]{:S(2)}, u32[]{:S(2)}) collective-permute-start(bf16[280,112]{1,0:T(8,128)(2,1)S(1)} %dynamic-slice_convert_fusion), channel_id=1, source_target_pairs={{0,4},{4,0},{1,5},{5,1},{2,6},{6,2},{3,7},{7,3},{8,12},{12,8},{9,1... | collective-permute-start | bytes 188168 | tf_op jit(solution)/shard_map/ppermute | solution.py:30
  6.0 0.9 collective-permute-done
  6.9 0.1 collective-permute-start.1
  7.0 1.9 %collective-permute-start.2 = (bf16[280,112]{1,0:T(8,128)(2,1)S(1)}, bf16[280,112]{1,0:T(8,128)(2,1)S(1)}, u32[]{:S(2)}, u32[]{:S(2)}) collective-permute-start(bf16[280,112]{1,0:T(8,128)(2,1)S(1)} %fusion.26), channel_id=1, source_target_pairs={{0,16},{8,24},{16,0},{24,8},{1,17},{9,25},{17,1},{25,9},{2,18},{10... | collective-permute-start | bytes 188168 | tf_op jit(solution)/shard_map/ppermute | solution.py:21
  8.9 1.2 %collective-permute-start.3 = (bf16[280,112]{1,0:T(8,128)(2,1)S(1)}, bf16[280,112]{1,0:T(8,128)(2,1)S(1)}, u32[]{:S(2)}, u32[]{:S(2)}) collective-permute-start(bf16[280,112]{1,0:T(8,128)(2,1)S(1)} %fusion.26), channel_id=1, source_target_pairs={{0,24},{8,0},{16,8},{24,16},{1,25},{9,1},{17,9},{25,17},{2,26},{10... | collective-permute-start | bytes 188168 | tf_op jit(solution)/shard_map/ppermute | solution.py:21
  10.1 2.2 %collective-permute-done.1 = bf16[280,112]{1,0:T(8,128)(2,1)S(1)} collective-permute-done((bf16[280,112]{1,0:T(8,128)(2,1)S(1)}, bf16[280,112]{1,0:T(8,128)(2,1)S(1)}, u32[]{:S(2)}, u32[]{:S(2)}) %collective-permute-start.1) | collective-permute-done | bytes 62752 | tf_op jit(solution)/shard_map/ppermute | solution.py:21
  12.3 0.5 collective-permute-done.2
  12.8 0.6 collective-permute-done.3
  13.4 0.1 fusion.34
  13.5 0.6 copy-done.6
  14.1 2.5 %collective-permute-start.4 = (bf16[280,112]{1,0:T(8,128)(2,1)S(1)}, bf16[280,112]{1,0:T(8,128)(2,1)S(1)}, u32[]{:S(2)}, u32[]{:S(2)}) collective-permute-start(bf16[280,112]{1,0:T(8,128)(2,1)S(1)} %get-tuple-element.7), channel_id=1, source_target_pairs={{0,32},{32,64},{64,96},{96,128},{128,160},{160,192},{192,224},{1,3... | collective-permute-start | bytes 188168 | tf_op jit(solution)/shard_map/ppermute | solution.py:16
  16.6 4.9 %collective-permute-start.5 = (bf16[280,112]{1,0:T(8,128)(2,1)S(1)}, bf16[280,112]{1,0:T(8,128)(2,1)S(1)}, u32[]{:S(2)}, u32[]{:S(2)}) collective-permute-start(bf16[280,112]{1,0:T(8,128)(2,1)S(1)} %get-tuple-element.7), channel_id=1, source_target_pairs={{0,64},{32,96},{64,128},{96,160},{128,192},{160,224},{1,65},{33,97... | collective-permute-start | bytes 188168 | tf_op jit(solution)/shard_map/ppermute | solution.py:16
  21.5 4.6 %collective-permute-start.9 = (bf16[5,112,880]{2,1,0:T(8,128)(2,1)}, bf16[5,112,880]{2,1,0:T(8,128)(2,1)}, u32[]{:S(2)}, u32[]{:S(2)}) collective-permute-start(bf16[5,112,880]{2,1,0:T(8,128)(2,1)} %bitcast.9), channel_id=1, source_target_pairs={{0,4},{4,8},{8,12},{12,16},{16,20},{20,24},{24,28},{28,32},{32,36}... | collective-permute-start | bytes 2956808 | tf_op jit(solution)/shard_map/ppermute | solution.py:16
  26.1 1.9 %collective-permute-start.11 = (bf16[5,112,880]{2,1,0:T(8,128)(2,1)}, bf16[5,112,880]{2,1,0:T(8,128)(2,1)}, u32[]{:S(2)}, u32[]{:S(2)}) collective-permute-start(bf16[5,112,880]{2,1,0:T(8,128)(2,1)} %bitcast.9), channel_id=1, source_target_pairs={{4,0},{8,4},{12,8},{16,12},{20,16},{24,20},{28,24},{32,28},{36,32}... | collective-permute-start | bytes 2956808 | tf_op jit(solution)/shard_map/ppermute | solution.py:16
  28.1 1.9 %collective-permute-start.10 = (bf16[5,112,112]{2,1,0:T(8,128)(2,1)}, bf16[5,112,112]{2,1,0:T(8,128)(2,1)}, u32[]{:S(2)}, u32[]{:S(2)}) collective-permute-start(bf16[5,112,112]{2,1,0:T(8,128)(2,1)} %get-tuple-element.15), channel_id=1, source_target_pairs={{4,0},{8,4},{12,8},{16,12},{20,16},{24,20},{28,24},{32,28},{36,32}... | collective-permute-start | bytes 376328 | tf_op jit(solution)/shard_map/ppermute | solution.py:16
  30.1 0.0 collective-permute-done.4
  30.1 0.0 collective-permute-done.5
  30.1 0.7 add_convert_fusion.2
  30.8 9.7 %collective-permute-start.6 = (bf16[280,112]{1,0:T(8,128)(2,1)}, bf16[280,112]{1,0:T(8,128)(2,1)}, u32[]{:S(2)}, u32[]{:S(2)}) collective-permute-start(bf16[280,112]{1,0:T(8,128)(2,1)} %add_convert_fusion.2), channel_id=1, source_target_pairs={{0,96},{32,128},{64,160},{96,192},{128,224},{1,97},{33,129},{65,16... | collective-permute-start | bytes 188168 | tf_op jit(solution)/shard_map/ppermute | solution.py:16
  40.5 1.9 %collective-permute-start.7 = (bf16[280,112]{1,0:T(8,128)(2,1)}, bf16[280,112]{1,0:T(8,128)(2,1)}, u32[]{:S(2)}, u32[]{:S(2)}) collective-permute-start(bf16[280,112]{1,0:T(8,128)(2,1)} %add_convert_fusion.2), channel_id=1, source_target_pairs={{0,192},{32,224},{1,193},{33,225},{2,194},{34,226},{3,195},{35,227... | collective-permute-start | bytes 188168 | tf_op jit(solution)/shard_map/ppermute | solution.py:16
  42.4 12.1 %dynamic-slice_bitcast_fusion.2 = (bf16[560,1680]{0,1:T(8,128)(2,1)}, bf16[560,1680]{0,1:T(8,128)(2,1)}, bf16[560,1680]{0,1:T(8,128)(2,1)}, bf16[560,1680]{0,1:T(8,128)(2,1)S(1)}) fusion(bf16[1680,2240]{1,0:T(8,128)(2,1)} %bitcast.43, s32[]{:T(128)S(6)} %select_n.93, s32[]{:T(128)S(6)} %select_n.97, s32[]{:T(128)S(6)} %select_n.95, s32[]{:T(128)S(6)} %select_n.78), kind=kLoop, calls=%fused_computation.3 | loop fusion | bytes 15052816 | tf_op jit(solution)/shard_map/transpose | solution.py:76
  54.4 0.0 collective-permute-done.6
  54.4 0.0 collective-permute-done.7
  54.4 1.2 %fusion.21 = (bf16[280,112]{1,0:T(8,128)(2,1)S(1)}, f32[280,112]{1,0:T(8,128)S(1)}) fusion(f32[560,112]{1,0:T(8,128)S(1)} %bitcast.47, s32[]{:T(128)S(6)} %select_n.81, pred[]{:T(512)S(6)} %eq.11, bf16[280,112]{1,0:T(8,128)(2,1)} %collective-permute-done.7, bf16[280,112]{1,0:T(8,128)(2,1)} %collective-permute-done.6, bf16[280,112]{1,0:T(8,128)(2,1)} %copy-done.8, ...), kind=kLoop, calls=%fused_computation.58 | loop fusion | flops 595840 | bytes 752648 | tf_op jit(solution)/shard_map/convert_element_type | solution.py:48
  55.6 0.6 collective-permute-start.8
  56.2 1.7 %bitcast_multiply_fusion = f32[560,880]{1,0:T(8,128)S(1)} fusion(bf16[880,560]{0,1:T(8,128)(2,1)} %param.9), kind=kLoop, calls=%fused_computation.5 | loop fusion | flops 2464000 | bytes 2956800 | tf_op jit(solution)/shard_map/jit(silu)/mul | solution.py:100
  57.9 0.0 collective-permute-done.8
  58.0 1.7 %multiply_reduce_fusion.1 = (f32[5,880]{1,0:T(8,128)S(1)}, f32[5,112,880]{2,1,0:T(8,128)S(1)}) fusion(bf16[5,112,880]{2,1,0:T(8,128)(2,1)} %bitcast.9, f32[5,112,112]{2,1,0:T(8,128)S(1)} %bitcast.48, f32[5,112,112]{2,1,0:T(8,128)S(1)} %get-tuple-element.16), kind=kOutput, calls=%fused_computation.13 | convolution fusion | flops 111986640 | bytes 3476160 | tf_op jit(solution)/shard_map/hab,hat->hbt/dot_general | solution.py:55
  59.8 0.1 multiply_convert_fusion.1
  59.9 0.0 collective-permute-done.9
  59.9 1.7 %multiply_reduce_fusion.2 = (f32[5,880]{1,0:T(8,128)S(1)}, f32[5,112,880]{2,1,0:T(8,128)S(1)}) fusion(bf16[5,112,880]{2,1,0:T(8,128)(2,1)} %collective-permute-done.9, f32[5,112,112]{2,1,0:T(8,128)S(1)} %bitcast.49), kind=kOutput, calls=%fused_computation.15 | convolution fusion | flops 111923920 | bytes 3225280 | tf_op jit(solution)/shard_map/hab,hat->hbt/dot_general | solution.py:55
  61.7 0.0 collective-permute-done.10
  61.7 0.0 collective-permute-done.11
  61.7 1.8 %multiply_reduce_fusion = (f32[5,880]{1,0:T(8,128)S(1)}, f32[5,112,880]{2,1,0:T(8,128)S(1)}) fusion(bf16[5,112,880]{2,1,0:T(8,128)(2,1)} %collective-permute-done.11, bf16[5,112,112]{2,1,0:T(8,128)(2,1)} %collective-permute-done.10, f32[5,112,112]{2,1,0:T(8,128)S(1)} %bitcast.50, f32[5,112,112]{2,1,0:T(8,128)S(1)} %get-tuple-element.16), kind=kOutput, calls=%fused_computation.11 | convolution fusion | flops 112112080 | bytes 3601600 | tf_op jit(solution)/shard_map/hab,hat->hbt/dot_general | solution.py:55
  63.5 0.1 multiply_convert_fusion.2
  63.6 0.0 copy-start.3
  63.7 0.1 multiply_convert_fusion
  63.8 1.4 %copy-done.3 = bf16[560,1680]{0,1:T(8,128)(2,1)S(1)} copy-done((bf16[560,1680]{0,1:T(8,128)(2,1)S(1)}, bf16[560,1680]{0,1:T(8,128)(2,1)}, u32[]{:S(2)}) %copy-start.3) | copy-done | bytes 1881624
  65.3 2.3 %convolution_convert_fusion = bf16[560,880]{1,0:T(8,128)(2,1)S(1)} fusion(bf16[560,1680]{0,1:T(8,128)(2,1)S(1)} %copy-done.3, bf16[560,880]{1,0:T(8,128)(2,1)S(1)} %bitcast.60, bf16[560,880]{1,0:T(8,128)(2,1)S(1)} %bitcast.52, bf16[560,880]{1,0:T(8,128)(2,1)S(1)} %bitcast.56), kind=kOutput, calls=%fused_computation.16 | convolution fusion | flops 1665171200 | bytes 5824000 | tf_op jit(solution)/shard_map/dot_general | solution.py:86
  67.7 2.3 %fusion.31 = f32[560,880]{1,0:T(8,128)S(1)} fusion(bf16[560,1680]{0,1:T(8,128)(2,1)S(1)} %copy-done.2, bf16[560,880]{1,0:T(8,128)(2,1)S(1)} %bitcast.61, bf16[560,880]{1,0:T(8,128)(2,1)S(1)} %bitcast.53, bf16[560,880]{1,0:T(8,128)(2,1)S(1)} %bitcast.57), kind=kOutput, calls=%fused_computation.74 | convolution fusion | flops 1664678400 | bytes 6809600 | tf_op jit(solution)/shard_map/dot_general | solution.py:86
  70.0 1.4 %collective-permute-start.12 = (bf16[288,880]{1,0:T(8,128)(2,1)S(1)}, bf16[288,880]{1,0:T(8,128)(2,1)S(1)}, u32[]{:S(2)}, u32[]{:S(2)}) collective-permute-start(bf16[288,880]{1,0:T(8,128)(2,1)S(1)} %slice.44), channel_id=1, source_target_pairs={{0,1},{1,2},{2,3},{3,0},{4,5},{5,6},{6,7},{7,4},{8,9},{9,10},{10,1... | collective-permute-start | bytes 1520648 | tf_op jit(solution)/shard_map/ppermute | solution.py:21
  71.3 1.5 %collective-permute-start.16 = (bf16[272,880]{1,0:T(8,128)(2,1)S(1)}, bf16[272,880]{1,0:T(8,128)(2,1)S(1)}, u32[]{:S(2)}, u32[]{:S(2)}) collective-permute-start(bf16[272,880]{1,0:T(8,128)(2,1)S(1)} %slice.50), channel_id=1, source_target_pairs={{0,3},{1,0},{2,1},{3,2},{4,7},{5,4},{6,5},{7,6},{8,11},{9,8},{10,9... | collective-permute-start | bytes 1436168 | tf_op jit(solution)/shard_map/ppermute | solution.py:21
  72.9 2.3 %fusion.30 = f32[560,880]{1,0:T(8,128)S(1)} fusion(bf16[560,1680]{0,1:T(8,128)(2,1)S(1)} %copy-done.1, bf16[560,880]{1,0:T(8,128)(2,1)S(1)} %bitcast.62, bf16[560,880]{1,0:T(8,128)(2,1)S(1)} %bitcast.54, bf16[560,880]{1,0:T(8,128)(2,1)S(1)} %bitcast.58), kind=kOutput, calls=%fused_computation.73 | convolution fusion | flops 1664678400 | bytes 6809600 | tf_op jit(solution)/shard_map/dot_general | solution.py:86
  75.1 0.1 slice.76
  75.2 1.4 %collective-permute-start.14 = (bf16[288,880]{1,0:T(8,128)(2,1)S(1)}, bf16[288,880]{1,0:T(8,128)(2,1)S(1)}, u32[]{:S(2)}, u32[]{:S(2)}) collective-permute-start(bf16[288,880]{1,0:T(8,128)(2,1)S(1)} %slice.76), channel_id=1, source_target_pairs={{0,3},{1,0},{2,1},{3,2},{4,7},{5,4},{6,5},{7,6},{8,11},{9,8},{10,9... | collective-permute-start | bytes 1520648 | tf_op jit(solution)/shard_map/ppermute | solution.py:21
  76.7 0.1 slice.77
  76.7 0.2 collective-permute-start.15
  76.9 6.6 %collective-permute-done.16 = bf16[272,880]{1,0:T(8,128)(2,1)S(1)} collective-permute-done((bf16[272,880]{1,0:T(8,128)(2,1)S(1)}, bf16[272,880]{1,0:T(8,128)(2,1)S(1)}, u32[]{:S(2)}, u32[]{:S(2)}) %collective-permute-start.16) | collective-permute-done | bytes 478752 | tf_op jit(solution)/shard_map/ppermute | solution.py:21
  83.5 0.1 fusion.13
  83.6 3.0 %collective-permute-start.17 = (bf16[272,880]{1,0:T(8,128)(2,1)S(1)}, bf16[272,880]{1,0:T(8,128)(2,1)S(1)}, u32[]{:S(2)}, u32[]{:S(2)}) collective-permute-start(bf16[272,880]{1,0:T(8,128)(2,1)S(1)} %fusion.13), channel_id=1, source_target_pairs={{0,3},{1,0},{2,1},{3,2},{4,7},{5,4},{6,5},{7,6},{8,11},{9,8},{10,9... | collective-permute-start | bytes 1436168 | tf_op jit(solution)/shard_map/ppermute | solution.py:21
  86.6 0.0 collective-permute-done.12
  86.6 0.1 fusion.4
  86.7 0.1 collective-permute-start.13
  86.8 2.3 %fusion.32 = f32[560,880]{1,0:T(8,128)S(1)} fusion(bf16[560,1680]{0,1:T(8,128)(2,1)S(1)} %get-tuple-element.12, bf16[560,880]{1,0:T(8,128)(2,1)S(1)} %bitcast.63, bf16[560,880]{1,0:T(8,128)(2,1)S(1)} %bitcast.55, bf16[560,880]{1,0:T(8,128)(2,1)S(1)} %bitcast.59), kind=kOutput, calls=%fused_computation.75 | convolution fusion | flops 1664678400 | bytes 6809600 | tf_op jit(solution)/shard_map/dot_general | solution.py:86
  89.1 5.8 %collective-permute-done.15 = bf16[272,880]{1,0:T(8,128)(2,1)S(1)} collective-permute-done((bf16[272,880]{1,0:T(8,128)(2,1)S(1)}, bf16[272,880]{1,0:T(8,128)(2,1)S(1)}, u32[]{:S(2)}, u32[]{:S(2)}) %collective-permute-start.15) | collective-permute-done | bytes 478752 | tf_op jit(solution)/shard_map/ppermute | solution.py:21
  94.9 10.1 %collective-permute-done.17 = bf16[272,880]{1,0:T(8,128)(2,1)S(1)} collective-permute-done((bf16[272,880]{1,0:T(8,128)(2,1)S(1)}, bf16[272,880]{1,0:T(8,128)(2,1)S(1)}, u32[]{:S(2)}, u32[]{:S(2)}) %collective-permute-start.17) | collective-permute-done | bytes 478752 | tf_op jit(solution)/shard_map/ppermute | solution.py:21
  105.0 0.2 fusion.12
  105.3 0.0 collective-permute-done.14
  105.3 0.7 collective-permute-done.13
  106.0 0.2 fusion.3
  106.2 1.0 maximum_bitcast_fusion
  (23 shorter events, 0.2 us)
Async XLA Ops:
  0.0 1.5 %copy-start = (bf16[880,560]{0,1:T(8,128)(2,1)S(1)}, bf16[880,560]{0,1:T(8,128)(2,1)}, u32[]{:S(2)}) copy-start(bf16[880,560]{0,1:T(8,128)(2,1)} %param.7) | copy-start | bytes 2956804
  2.7 4.2 %collective-permute-start = (bf16[280,112]{1,0:T(8,128)(2,1)S(1)}, bf16[280,112]{1,0:T(8,128)(2,1)S(1)}, u32[]{:S(2)}, u32[]{:S(2)}) collective-permute-start(bf16[280,112]{1,0:T(8,128)(2,1)S(1)} %dynamic-slice_convert_fusion), channel_id=1, source_target_pairs={{0,4},{4,0},{1,5},{5,1},{2,6},{6,2},{3,7},{7,3},{8,12},{12,8},{9,1... | collective-permute-start | bytes 188168 | tf_op jit(solution)/shard_map/ppermute | solution.py:30
  6.9 5.4 %collective-permute-start.1 = (bf16[280,112]{1,0:T(8,128)(2,1)S(1)}, bf16[280,112]{1,0:T(8,128)(2,1)S(1)}, u32[]{:S(2)}, u32[]{:S(2)}) collective-permute-start(bf16[280,112]{1,0:T(8,128)(2,1)S(1)} %fusion.26), channel_id=1, source_target_pairs={{0,8},{8,16},{16,24},{24,0},{1,9},{9,17},{17,25},{25,1},{2,10},{10... | collective-permute-start | bytes 188168 | tf_op jit(solution)/shard_map/ppermute | solution.py:21
  7.0 5.8 %collective-permute-start.2 = (bf16[280,112]{1,0:T(8,128)(2,1)S(1)}, bf16[280,112]{1,0:T(8,128)(2,1)S(1)}, u32[]{:S(2)}, u32[]{:S(2)}) collective-permute-start(bf16[280,112]{1,0:T(8,128)(2,1)S(1)} %fusion.26), channel_id=1, source_target_pairs={{0,16},{8,24},{16,0},{24,8},{1,17},{9,25},{17,1},{25,9},{2,18},{10... | collective-permute-start | bytes 188168 | tf_op jit(solution)/shard_map/ppermute | solution.py:21
  8.9 4.5 %collective-permute-start.3 = (bf16[280,112]{1,0:T(8,128)(2,1)S(1)}, bf16[280,112]{1,0:T(8,128)(2,1)S(1)}, u32[]{:S(2)}, u32[]{:S(2)}) collective-permute-start(bf16[280,112]{1,0:T(8,128)(2,1)S(1)} %fusion.26), channel_id=1, source_target_pairs={{0,24},{8,0},{16,8},{24,16},{1,25},{9,1},{17,9},{25,17},{2,26},{10... | collective-permute-start | bytes 188168 | tf_op jit(solution)/shard_map/ppermute | solution.py:21
  12.3 1.2 %copy-start.4 = (bf16[280,112]{1,0:T(8,128)(2,1)}, bf16[280,112]{1,0:T(8,128)(2,1)S(1)}, u32[]{:S(2)}) copy-start(bf16[280,112]{1,0:T(8,128)(2,1)S(1)} %collective-permute-done.1) | copy-start | bytes 188164
  12.8 0.7 copy-start.5
  13.4 0.6 copy-start.6
  14.1 16.0 %collective-permute-start.4 = (bf16[280,112]{1,0:T(8,128)(2,1)S(1)}, bf16[280,112]{1,0:T(8,128)(2,1)S(1)}, u32[]{:S(2)}, u32[]{:S(2)}) collective-permute-start(bf16[280,112]{1,0:T(8,128)(2,1)S(1)} %get-tuple-element.7), channel_id=1, source_target_pairs={{0,32},{32,64},{64,96},{96,128},{128,160},{160,192},{192,224},{1,3... | collective-permute-start | bytes 188168 | tf_op jit(solution)/shard_map/ppermute | solution.py:16
  16.6 13.5 %collective-permute-start.5 = (bf16[280,112]{1,0:T(8,128)(2,1)S(1)}, bf16[280,112]{1,0:T(8,128)(2,1)S(1)}, u32[]{:S(2)}, u32[]{:S(2)}) collective-permute-start(bf16[280,112]{1,0:T(8,128)(2,1)S(1)} %get-tuple-element.7), channel_id=1, source_target_pairs={{0,64},{32,96},{64,128},{96,160},{128,192},{160,224},{1,65},{33,97... | collective-permute-start | bytes 188168 | tf_op jit(solution)/shard_map/ppermute | solution.py:16
  21.5 38.5 %collective-permute-start.9 = (bf16[5,112,880]{2,1,0:T(8,128)(2,1)}, bf16[5,112,880]{2,1,0:T(8,128)(2,1)}, u32[]{:S(2)}, u32[]{:S(2)}) collective-permute-start(bf16[5,112,880]{2,1,0:T(8,128)(2,1)} %bitcast.9), channel_id=1, source_target_pairs={{0,4},{4,8},{8,12},{12,16},{16,20},{20,24},{24,28},{28,32},{32,36}... | collective-permute-start | bytes 2956808 | tf_op jit(solution)/shard_map/ppermute | solution.py:16
  26.1 35.5 %collective-permute-start.11 = (bf16[5,112,880]{2,1,0:T(8,128)(2,1)}, bf16[5,112,880]{2,1,0:T(8,128)(2,1)}, u32[]{:S(2)}, u32[]{:S(2)}) collective-permute-start(bf16[5,112,880]{2,1,0:T(8,128)(2,1)} %bitcast.9), channel_id=1, source_target_pairs={{4,0},{8,4},{12,8},{16,12},{20,16},{24,20},{28,24},{32,28},{36,32}... | collective-permute-start | bytes 2956808 | tf_op jit(solution)/shard_map/ppermute | solution.py:16
  28.1 33.6 %collective-permute-start.10 = (bf16[5,112,112]{2,1,0:T(8,128)(2,1)}, bf16[5,112,112]{2,1,0:T(8,128)(2,1)}, u32[]{:S(2)}, u32[]{:S(2)}) collective-permute-start(bf16[5,112,112]{2,1,0:T(8,128)(2,1)} %get-tuple-element.15), channel_id=1, source_target_pairs={{4,0},{8,4},{12,8},{16,12},{20,16},{24,20},{28,24},{32,28},{36,32}... | collective-permute-start | bytes 376328 | tf_op jit(solution)/shard_map/ppermute | solution.py:16
  30.1 12.3 %copy-start.7 = (bf16[280,112]{1,0:T(8,128)(2,1)}, bf16[280,112]{1,0:T(8,128)(2,1)S(1)}, u32[]{:S(2)}) copy-start(bf16[280,112]{1,0:T(8,128)(2,1)S(1)} %collective-permute-done.4) | copy-start | bytes 188164
  30.1 12.3 %copy-start.8 = (bf16[280,112]{1,0:T(8,128)(2,1)}, bf16[280,112]{1,0:T(8,128)(2,1)S(1)}, u32[]{:S(2)}) copy-start(bf16[280,112]{1,0:T(8,128)(2,1)S(1)} %collective-permute-done.5) | copy-start | bytes 188164
  30.8 23.7 %collective-permute-start.6 = (bf16[280,112]{1,0:T(8,128)(2,1)}, bf16[280,112]{1,0:T(8,128)(2,1)}, u32[]{:S(2)}, u32[]{:S(2)}) collective-permute-start(bf16[280,112]{1,0:T(8,128)(2,1)} %add_convert_fusion.2), channel_id=1, source_target_pairs={{0,96},{32,128},{64,160},{96,192},{128,224},{1,97},{33,129},{65,16... | collective-permute-start | bytes 188168 | tf_op jit(solution)/shard_map/ppermute | solution.py:16
  40.5 14.0 %collective-permute-start.7 = (bf16[280,112]{1,0:T(8,128)(2,1)}, bf16[280,112]{1,0:T(8,128)(2,1)}, u32[]{:S(2)}, u32[]{:S(2)}) collective-permute-start(bf16[280,112]{1,0:T(8,128)(2,1)} %add_convert_fusion.2), channel_id=1, source_target_pairs={{0,192},{32,224},{1,193},{33,225},{2,194},{34,226},{3,195},{35,227... | collective-permute-start | bytes 188168 | tf_op jit(solution)/shard_map/ppermute | solution.py:16
  55.6 2.3 %collective-permute-start.8 = (bf16[280,112]{1,0:T(8,128)(2,1)S(1)}, bf16[280,112]{1,0:T(8,128)(2,1)S(1)}, u32[]{:S(2)}, u32[]{:S(2)}) collective-permute-start(bf16[280,112]{1,0:T(8,128)(2,1)S(1)} %get-tuple-element.5), channel_id=1, source_target_pairs={{0,4},{4,0},{1,5},{5,1},{2,6},{6,2},{3,7},{7,3},{8,12},{12,8},{9,1... | collective-permute-start | bytes 188168 | tf_op jit(solution)/shard_map/ppermute | solution.py:48
  63.6 1.6 %copy-start.3 = (bf16[560,1680]{0,1:T(8,128)(2,1)S(1)}, bf16[560,1680]{0,1:T(8,128)(2,1)}, u32[]{:S(2)}) copy-start(bf16[560,1680]{0,1:T(8,128)(2,1)} %get-tuple-element.11) | copy-start | bytes 5644804
  65.3 2.4 %copy-start.2 = (bf16[560,1680]{0,1:T(8,128)(2,1)S(1)}, bf16[560,1680]{0,1:T(8,128)(2,1)}, u32[]{:S(2)}) copy-start(bf16[560,1680]{0,1:T(8,128)(2,1)} %get-tuple-element.9) | copy-start | bytes 5644804
  67.7 5.2 %copy-start.1 = (bf16[560,1680]{0,1:T(8,128)(2,1)S(1)}, bf16[560,1680]{0,1:T(8,128)(2,1)}, u32[]{:S(2)}) copy-start(bf16[560,1680]{0,1:T(8,128)(2,1)} %get-tuple-element.10) | copy-start | bytes 5644804
  70.0 16.7 %collective-permute-start.12 = (bf16[288,880]{1,0:T(8,128)(2,1)S(1)}, bf16[288,880]{1,0:T(8,128)(2,1)S(1)}, u32[]{:S(2)}, u32[]{:S(2)}) collective-permute-start(bf16[288,880]{1,0:T(8,128)(2,1)S(1)} %slice.44), channel_id=1, source_target_pairs={{0,1},{1,2},{2,3},{3,0},{4,5},{5,6},{6,7},{7,4},{8,9},{9,10},{10,1... | collective-permute-start | bytes 1520648 | tf_op jit(solution)/shard_map/ppermute | solution.py:21
  71.3 12.2 %collective-permute-start.16 = (bf16[272,880]{1,0:T(8,128)(2,1)S(1)}, bf16[272,880]{1,0:T(8,128)(2,1)S(1)}, u32[]{:S(2)}, u32[]{:S(2)}) collective-permute-start(bf16[272,880]{1,0:T(8,128)(2,1)S(1)} %slice.50), channel_id=1, source_target_pairs={{0,3},{1,0},{2,1},{3,2},{4,7},{5,4},{6,5},{7,6},{8,11},{9,8},{10,9... | collective-permute-start | bytes 1436168 | tf_op jit(solution)/shard_map/ppermute | solution.py:21
  75.2 30.1 %collective-permute-start.14 = (bf16[288,880]{1,0:T(8,128)(2,1)S(1)}, bf16[288,880]{1,0:T(8,128)(2,1)S(1)}, u32[]{:S(2)}, u32[]{:S(2)}) collective-permute-start(bf16[288,880]{1,0:T(8,128)(2,1)S(1)} %slice.76), channel_id=1, source_target_pairs={{0,3},{1,0},{2,1},{3,2},{4,7},{5,4},{6,5},{7,6},{8,11},{9,8},{10,9... | collective-permute-start | bytes 1520648 | tf_op jit(solution)/shard_map/ppermute | solution.py:21
  76.7 18.2 %collective-permute-start.15 = (bf16[272,880]{1,0:T(8,128)(2,1)S(1)}, bf16[272,880]{1,0:T(8,128)(2,1)S(1)}, u32[]{:S(2)}, u32[]{:S(2)}) collective-permute-start(bf16[272,880]{1,0:T(8,128)(2,1)S(1)} %slice.77), channel_id=1, source_target_pairs={{0,1},{1,2},{2,3},{3,0},{4,5},{5,6},{6,7},{7,4},{8,9},{9,10},{10,1... | collective-permute-start | bytes 1436168 | tf_op jit(solution)/shard_map/ppermute | solution.py:21
  83.6 21.4 %collective-permute-start.17 = (bf16[272,880]{1,0:T(8,128)(2,1)S(1)}, bf16[272,880]{1,0:T(8,128)(2,1)S(1)}, u32[]{:S(2)}, u32[]{:S(2)}) collective-permute-start(bf16[272,880]{1,0:T(8,128)(2,1)S(1)} %fusion.13), channel_id=1, source_target_pairs={{0,3},{1,0},{2,1},{3,2},{4,7},{5,4},{6,5},{7,6},{8,11},{9,8},{10,9... | collective-permute-start | bytes 1436168 | tf_op jit(solution)/shard_map/ppermute | solution.py:21
  86.7 19.2 %collective-permute-start.13 = (bf16[288,880]{1,0:T(8,128)(2,1)S(1)}, bf16[288,880]{1,0:T(8,128)(2,1)S(1)}, u32[]{:S(2)}, u32[]{:S(2)}) collective-permute-start(bf16[288,880]{1,0:T(8,128)(2,1)S(1)} %fusion.4), channel_id=1, source_target_pairs={{0,1},{1,2},{2,3},{3,0},{4,5},{5,6},{6,7},{7,4},{8,9},{9,10},{10,1... | collective-permute-start | bytes 1520648 | tf_op jit(solution)/shard_map/ppermute | solution.py:21

commit v2 on v1

v2 whole, which is shorter than its diff:
```python
import jax
import jax.numpy as jnp
from jax import lax
from jax.sharding import Mesh, PartitionSpec as P


HD = 112
TPF = 880
BF = jnp.bfloat16
F32 = jnp.float32
NZ, NX, NC, NY = 8, 4, 2, 4
FR = ("z", "x", "c")


def ring(value, axis, step):
    count = lax.axis_size(axis)
    return lax.ppermute(value, axis, [(i, (i + step) % count) for i in range(count)])


def after(value, anchor):
    return lax.optimization_barrier((value, anchor))[0]


def earlier_frames(state, slice_weights):
    half = state.shape[0] // 2
    core = lax.axis_index("c")
    x_at = lax.axis_index("x")
    mine = lax.dynamic_slice_in_dim(state, core * half, half, 0)
    other = lax.dynamic_slice_in_dim(state, (1 - core) * half, half, 0)
    theirs = ring(other.astype(BF), "c", 1).astype(F32)
    chip = mine + theirs
    chip_bf = chip.astype(BF)
    total, before = chip, jnp.zeros_like(chip)
    for step in (1, 2, 3):
        got = ring(chip_bf, "x", step).astype(F32)
        total = total + got
        before = before + jnp.where(x_at >= step, got, 0.0)
    total_bf = total.astype(BF)
    taps = {2: slice_weights(2, chip_bf), 1: slice_weights(1, total_bf)}
    z_at = lax.axis_index("z")
    last = lax.axis_size("z") - 1
    below = jnp.where(z_at >= 1, ring(total_bf, "z", 1).astype(F32), 0.0)
    above = ring(total_bf, "z", -1).astype(F32)
    for_up = (above + jnp.where(z_at == last, 0.0, total + below)).astype(BF)
    for_down = (total + below).astype(BF)
    taps[3] = slice_weights(3, for_up)
    from_below = jnp.where(z_at >= 2, ring(for_up, "z", 3).astype(F32), 0.0)
    from_above = jnp.where(z_at >= 5, ring(for_down, "z", -3).astype(F32), 0.0)
    before = before + (below + jnp.where(z_at == last, above, 0.0) + (from_below + from_above))
    to_other = jnp.where(core == 0, before + mine, before)
    to_self = jnp.where(core == 0, before, before + theirs)
    from_other = ring(to_other.astype(BF), "c", 1).astype(F32)
    first = jnp.where(core == 0, to_self, from_other)
    second = jnp.where(core == 0, from_other, to_self)
    return jnp.concatenate([first, second], axis=0), taps


def attend(query, prefix):
    readout = jnp.einsum("hab,hat->hbt", prefix, jnp.maximum(query, 0), preferred_element_type=F32)
    scale = lax.rsqrt(jnp.mean(readout * readout, axis=1, keepdims=True) + 1e-06)
    return (readout * scale).astype(BF).reshape(-1, query.shape[-1])


def shards(query_act, key_act, value_act, conv_weight, gate_act):
    heads = query_act.shape[1] // HD
    width = heads * HD
    turned = lambda a: a.T.reshape(heads, HD, TPF)
    query = turned(query_act)
    q_prev = ring(query, FR, 1)
    q_next = ring(query, FR, -1)
    key = jnp.maximum(turned(key_act), 0)
    state = jnp.einsum("hat,hbt->hab", key, turned(value_act), preferred_element_type=F32)
    s_next = ring(state.astype(BF), FR, -1).astype(F32)
    me = lax.axis_index("y")
    frame, frames = lax.axis_index(FR), lax.axis_size(FR)
    flat = conv_weight.reshape(3 * width, NY * width)

    def slice_weights(away, anchor):
        return lax.dynamic_slice_in_dim(flat, ((me + away) % NY) * width, width, 1)

    earlier, taps = earlier_frames(state.reshape(width, HD), slice_weights)
    earlier = earlier.reshape(state.shape)
    here = earlier + state
    own_att = attend(query, here.astype(BF))
    att = jnp.concatenate(
        [
            attend(q_prev, earlier.astype(BF)),
            own_att,
            attend(q_next, jnp.where(frame < frames - 1, here + s_next, 0.0).astype(BF)),
        ],
        axis=0,
    )

    def part(away, dtype):
        weights = taps[away] if away in taps else slice_weights(away, far)
        return lax.dot_general(weights, att, (((0,), (0,)), ((), ())), preferred_element_type=F32).astype(dtype)

    cut = (width // 2 + 15) // 16 * 16
    far = part(2, BF)
    a_up = ring(far[:cut], "y", 1)
    a_down = ring(far[cut:], "y", -1)
    up = part(1, F32)
    down = part(3, F32)
    b_up = ring(up[cut:].astype(BF), "y", 1)
    b_down = ring(down[:cut].astype(BF), "y", -1)
    own = part(0, F32)
    c_up = ring((up[:cut] + a_up.astype(F32)).astype(BF), "y", 1)
    c_down = ring((down[cut:] + a_down.astype(F32)).astype(BF), "y", -1)
    gate = jax.nn.silu(after(gate_act, far).T.astype(F32))
    top = own[:cut] + c_up.astype(F32) + b_down.astype(F32)
    bottom = own[cut:] + b_up.astype(F32) + c_down.astype(F32)
    out = jnp.concatenate([(top * gate[:cut]).astype(BF), (bottom * gate[cut:]).astype(BF)], axis=0)
    return out.T


def solution(mesh):
    fine = Mesh(mesh.devices.reshape(NZ, NX, NC, NY), FR + ("y",))
    act = P(FR, "y")

    return jax.shard_map(
        shards,
        mesh=fine,
        in_specs=(act, act, act, P(None, "y", None), act),
        out_specs=act,
        check_vma=False,
    )
```

time: 108 us -> 98.3 us (0.910)
  waiting for transfers between devices: 27.5 us -> 45.9 us
  local copies, waits for them, and re-layouts: 14.4 us -> 1.5 us
  starting transfers between devices: 42.1 us -> 30.3 us
  matrix products: 15.5 us -> 14.1 us
  other arithmetic: 7.34 us -> 6 us
    ppermute x9 -> x0, starting transfers between devices: 31.3 us -> none  [the longest x7 27.5 us: shift(): lax.ppermute(value, axis, [(i, i + step) for i in range(count) if 0 <= i...]
    ppermute x9 -> x18, starting transfers between devices: 10.7 us -> 30.3 us  [ring(): lax.ppermute(value, axis, [(i, (i + step) % count) for i in range(count)])]
    ppermute x9 -> x18, waiting for transfers between devices: 26.6 us -> 45.9 us  [ring(): lax.ppermute(value, axis, [(i, (i + step) % count) for i in range(count)])]
    transpose x1 -> x0, local copies, waits for them, and re-layouts: 12.1 us -> none  [shards(): taps.append(lax.optimization_barrier(piece.T))]
    dot_general x3, matrix products: 5.21 us -> 2.79 us  [attend(): jnp.einsum('hab,hat->hbt', prefix, jnp.maximum(query, 0), preferred_eleme...]
    mul x1, other arithmetic: 1.74 us -> 0.53 us  [shards(): gate = jax.nn.silu(after(gate_act, far).T.astype(F32))]
  transfers between devices with their start and end apart: 18 -> 18, of which waited for: 8 -> 12; matrix products, arithmetic and copies ran while one was open for 23% -> 12% of each run, Pallas kernels for 0% -> 0%
where the time goes in v2:
time: 98.3 us; the launch traced here: 98.1 us
  waiting for transfers between devices  45.9 us (47%)
  starting transfers between devices  30.3 us (31%)
  matrix products  14.1 us (14%)
  other arithmetic  6 us (6%)
  local copies, waits for them, and re-layouts  1.5 us (2%)
    ppermute x18, waiting for transfers between devices, ring(): lax.ppermute(value, axis, [(i, (i + step) % count) for i in range(count)])  45.9 us
    ppermute x18, starting transfers between devices, ring(): lax.ppermute(value, axis, [(i, (i + step) % count) for i in range(count)])  30.3 us
    dot_general x4, matrix products, part(): lax.dot_general(weights, att, (((0,), (0,)), ((), ())), preferred_element...  10.2 us
    dot_general x3, matrix products, attend(): jnp.einsum('hab,hat->hbt', prefix, jnp.maximum(query, 0), preferred_eleme...  2.79 us
  transfers between devices with their start and end apart: 18, of which 12 were waited for; matrix products, arithmetic and copies ran while one was open for 12% of the time, Pallas kernels for 0%

profile of v2, /device:TPU:1, one launch (start us, length us, event | category | flops | bytes accessed | tf_op | source)
XLA Modules:
  0.0 98.1 jit_solution(13924377490320733234)
XLA Ops:
  0.0 1.4 %broadcast_maximum_fusion = bf16[880,560]{0,1:T(8,128)(2,1)S(1)} fusion(bf16[880,560]{0,1:T(8,128)(2,1)} %param.6), kind=kLoop, calls=%fused_computation.45 | loop fusion | flops 492800 | bytes 1971200 | tf_op jit(solution)/shard_map/max | solution.py:71
  1.4 0.1 copy-done
  1.5 1.1 %fusion.55 = (bf16[5,112,112]{2,1,0:T(8,128)(2,1)}, f32[5,112,112]{2,1,0:T(8,128)S(1)}) fusion(bf16[5,112,880]{2,1,0:T(8,128)(2,1)S(1)} %bitcast.38, bf16[5,112,880]{2,1,0:T(8,128)(2,1)S(1)} %bitcast.30), kind=kOutput, calls=%fused_computation.91 | convolution fusion | flops 110449920 | bytes 2347520 | tf_op jit(solution)/shard_map/hat,hbt->hab/dot_general | solution.py:72
  2.7 3.3 %collective-permute-start = (bf16[280,112]{1,0:T(8,128)(2,1)S(1)}, bf16[280,112]{1,0:T(8,128)(2,1)S(1)}, u32[]{:S(2)}, u32[]{:S(2)}) collective-permute-start(bf16[280,112]{1,0:T(8,128)(2,1)S(1)} %dynamic-slice_convert_fusion), channel_id=1, source_target_pairs={{0,4},{4,0},{1,5},{5,1},{2,6},{6,2},{3,7},{7,3},{8,12},{12,8},{9,1... | collective-permute-start | bytes 188168 | tf_op jit(solution)/shard_map/ppermute | solution.py:17
  6.0 0.9 collective-permute-done
  6.9 0.8 collective-permute-start.3
  7.7 0.5 collective-permute-start.2
  8.3 0.6 collective-permute-start.1
  8.9 1.3 %collective-permute-done.3 = bf16[280,112]{1,0:T(8,128)(2,1)S(1)} collective-permute-done((bf16[280,112]{1,0:T(8,128)(2,1)S(1)}, bf16[280,112]{1,0:T(8,128)(2,1)S(1)}, u32[]{:S(2)}, u32[]{:S(2)}) %collective-permute-start.3) | collective-permute-done | bytes 62752 | tf_op jit(solution)/shard_map/ppermute | solution.py:17
  10.1 2.3 %collective-permute-done.2 = bf16[280,112]{1,0:T(8,128)(2,1)S(1)} collective-permute-done((bf16[280,112]{1,0:T(8,128)(2,1)S(1)}, bf16[280,112]{1,0:T(8,128)(2,1)S(1)}, u32[]{:S(2)}, u32[]{:S(2)}) %collective-permute-start.2) | collective-permute-done | bytes 62752 | tf_op jit(solution)/shard_map/ppermute | solution.py:17
  12.5 2.1 %collective-permute-done.1 = bf16[280,112]{1,0:T(8,128)(2,1)S(1)} collective-permute-done((bf16[280,112]{1,0:T(8,128)(2,1)S(1)}, bf16[280,112]{1,0:T(8,128)(2,1)S(1)}, u32[]{:S(2)}, u32[]{:S(2)}) %collective-permute-start.1) | collective-permute-done | bytes 62752 | tf_op jit(solution)/shard_map/ppermute | solution.py:17
  14.5 0.1 fusion.54
  14.6 5.5 %collective-permute-start.5 = (bf16[280,112]{1,0:T(8,128)(2,1)S(1)}, bf16[280,112]{1,0:T(8,128)(2,1)S(1)}, u32[]{:S(2)}, u32[]{:S(2)}) collective-permute-start(bf16[280,112]{1,0:T(8,128)(2,1)S(1)} %get-tuple-element.9), channel_id=1, source_target_pairs={{0,224},{32,0},{64,32},{96,64},{128,96},{160,128},{192,160},{224,1... | collective-permute-start | bytes 188168 | tf_op jit(solution)/shard_map/ppermute | solution.py:17
  20.1 0.0 collective-permute-start.4
  20.1 1.4 %collective-permute-done.5 = bf16[280,112]{1,0:T(8,128)(2,1)S(1)} collective-permute-done((bf16[280,112]{1,0:T(8,128)(2,1)S(1)}, bf16[280,112]{1,0:T(8,128)(2,1)S(1)}, u32[]{:S(2)}, u32[]{:S(2)}) %collective-permute-start.5) | collective-permute-done | bytes 62752 | tf_op jit(solution)/shard_map/ppermute | solution.py:17
  21.5 3.0 %collective-permute-done.4 = bf16[280,112]{1,0:T(8,128)(2,1)S(1)} collective-permute-done((bf16[280,112]{1,0:T(8,128)(2,1)S(1)}, bf16[280,112]{1,0:T(8,128)(2,1)S(1)}, u32[]{:S(2)}, u32[]{:S(2)}) %collective-permute-start.4) | collective-permute-done | bytes 62752 | tf_op jit(solution)/shard_map/ppermute | solution.py:17
  24.6 0.1 collective-permute-start.6
  24.7 4.5 %collective-permute-start.7 = (bf16[280,112]{1,0:T(8,128)(2,1)S(1)}, bf16[280,112]{1,0:T(8,128)(2,1)S(1)}, u32[]{:S(2)}, u32[]{:S(2)}) collective-permute-start(bf16[280,112]{1,0:T(8,128)(2,1)S(1)} %get-tuple-element.14), channel_id=1, source_target_pairs={{0,160},{32,192},{64,224},{96,0},{128,32},{160,64},{192,96},{224,1... | collective-permute-start | bytes 188168 | tf_op jit(solution)/shard_map/ppermute | solution.py:17
  29.1 2.8 %collective-permute-done.6 = bf16[280,112]{1,0:T(8,128)(2,1)S(1)} collective-permute-done((bf16[280,112]{1,0:T(8,128)(2,1)S(1)}, bf16[280,112]{1,0:T(8,128)(2,1)S(1)}, u32[]{:S(2)}, u32[]{:S(2)}) %collective-permute-start.6) | collective-permute-done | bytes 62752 | tf_op jit(solution)/shard_map/ppermute | solution.py:17
  31.9 0.0 collective-permute-done.7
  31.9 0.7 fusion.35
  32.7 3.7 %collective-permute-start.8 = (bf16[280,112]{1,0:T(8,128)(2,1)}, bf16[280,112]{1,0:T(8,128)(2,1)}, u32[]{:S(2)}, u32[]{:S(2)}) collective-permute-start(bf16[280,112]{1,0:T(8,128)(2,1)} %get-tuple-element.7), channel_id=1, source_target_pairs={{0,4},{4,0},{1,5},{5,1},{2,6},{6,2},{3,7},{7,3},{8,12},{12,8},{9,1... | collective-permute-start | bytes 188168 | tf_op jit(solution)/shard_map/ppermute | solution.py:17
  36.3 0.0 collective-permute-start.11
  36.4 1.7 %collective-permute-start.9 = (bf16[5,112,880]{2,1,0:T(8,128)(2,1)S(1)}, bf16[5,112,880]{2,1,0:T(8,128)(2,1)S(1)}, u32[]{:S(2)}, u32[]{:S(2)}) collective-permute-start(bf16[5,112,880]{2,1,0:T(8,128)(2,1)S(1)} %bitcast.40), channel_id=1, source_target_pairs={{0,4},{4,8},{8,12},{12,16},{16,20},{20,24},{24,28},{28,32},{32,36}... | collective-permute-start | bytes 2956808 | tf_op jit(solution)/shard_map/ppermute | solution.py:17
  38.1 0.0 collective-permute-start.10
  38.1 0.0 collective-permute-done.8
  38.1 0.9 convert_select_fusion.1
  39.1 0.5 multiply_reduce_fusion.1
  39.6 0.0 slice-start
  39.6 0.1 multiply_convert_fusion.1
  39.7 12.2 %collective-permute-done.10 = bf16[5,112,112]{2,1,0:T(8,128)(2,1)} collective-permute-done((bf16[5,112,112]{2,1,0:T(8,128)(2,1)}, bf16[5,112,112]{2,1,0:T(8,128)(2,1)}, u32[]{:S(2)}, u32[]{:S(2)}) %collective-permute-start.10) | collective-permute-done | bytes 125472 | tf_op jit(solution)/shard_map/ppermute | solution.py:17
  51.9 0.0 collective-permute-done.11
  51.9 1.8 %multiply_reduce_fusion = (f32[5,880]{1,0:T(8,128)S(1)}, f32[5,112,880]{2,1,0:T(8,128)S(1)}) fusion(bf16[5,112,880]{2,1,0:T(8,128)(2,1)} %collective-permute-done.11, bf16[5,112,112]{2,1,0:T(8,128)(2,1)} %collective-permute-done.10, pred[]{:T(512)S(6)} %lt.43, f32[5,112,112]{2,1,0:T(8,128)S(1)} %bitcast.36, f32[5,112,112]{2,1,0:T(8,128)S(1)} %get-tuple-element.16), kind=kOutput, calls=%fused_computation.15 | convolution fusion | flops 112174800 | bytes 3601601 | tf_op jit(solution)/shard_map/hab,hat->hbt/dot_general | solution.py:59
  53.8 0.0 slice-start.1
  53.8 0.0 collective-permute-done.9
  53.8 0.5 multiply_reduce_fusion.2
  54.3 0.2 multiply_convert_fusion
  54.5 0.2 multiply_convert_fusion.2
  54.6 1.1 %slice-done.1 = s8[3547136]{0:T(1024)(128)(4,1)S(1)} async-done(((s8[7741440]{0:T(1024)(128)(4,1)}), s8[3547136]{0:T(1024)(128)(4,1)S(1)}, s32[]{:S(2)}) %slice-start.1) | async-done | bytes 3547160
  55.8 2.5 %fusion.11 = bf16[560,880]{1,0:T(8,128)(2,1)S(1)} fusion(bf16[1680,2240]{1,0:T(8,128)(2,1)S(1)} %bitcast.56, s32[]{:T(128)S(6)} %select_n.144, bf16[560,880]{1,0:T(8,128)(2,1)S(1)} %bitcast.46, bf16[560,880]{1,0:T(8,128)(2,1)S(1)} %bitcast.42, bf16[560,880]{1,0:T(8,128)(2,1)S(1)} %bitcast.50), kind=kOutput, calls=%fused_computation.20 | convolution fusion | flops 1665171200 | bytes 6146564 | tf_op jit(solution)/shard_map/dot_general | solution.py:96
  58.4 2.8 %collective-permute-start.16 = (bf16[272,880]{1,0:T(8,128)(2,1)S(1)}, bf16[272,880]{1,0:T(8,128)(2,1)S(1)}, u32[]{:S(2)}, u32[]{:S(2)}) collective-permute-start(bf16[272,880]{1,0:T(8,128)(2,1)S(1)} %slice.50), channel_id=1, source_target_pairs={{0,3},{1,0},{2,1},{3,2},{4,7},{5,4},{6,5},{7,6},{8,11},{9,8},{10,9... | collective-permute-start | bytes 1436168 | tf_op jit(solution)/shard_map/ppermute | solution.py:17
  61.2 0.0 collective-permute-start.12
  61.2 2.6 %fusion.4 = f32[560,880]{1,0:T(8,128)S(1)} fusion(bf16[1680,2240]{1,0:T(8,128)(2,1)S(1)} %bitcast.57, s32[]{:T(128)S(6)} %select_n.142, bf16[560,880]{1,0:T(8,128)(2,1)S(1)} %bitcast.47, bf16[560,880]{1,0:T(8,128)(2,1)S(1)} %bitcast.43, bf16[560,880]{1,0:T(8,128)(2,1)S(1)} %bitcast.51), kind=kOutput, calls=%fused_computation.5 | convolution fusion | flops 1664678400 | bytes 7132164 | tf_op jit(solution)/shard_map/dot_general | solution.py:96
  63.8 0.1 slice.77
  63.9 0.1 collective-permute-start.15
  64.0 2.6 %fusion = f32[560,880]{1,0:T(8,128)S(1)} fusion(bf16[1680,2240]{1,0:T(8,128)(2,1)S(1)} %bitcast.58, s32[]{:T(128)S(6)} %select_n.146, bf16[560,880]{1,0:T(8,128)(2,1)S(1)} %bitcast.48, bf16[560,880]{1,0:T(8,128)(2,1)S(1)} %bitcast.44, bf16[560,880]{1,0:T(8,128)(2,1)S(1)} %bitcast.52), kind=kOutput, calls=%fused_computation.1 | convolution fusion | flops 1664678400 | bytes 7132164 | tf_op jit(solution)/shard_map/dot_general | solution.py:96
  66.5 0.1 slice.76
  66.6 3.0 %collective-permute-start.14 = (bf16[288,880]{1,0:T(8,128)(2,1)S(1)}, bf16[288,880]{1,0:T(8,128)(2,1)S(1)}, u32[]{:S(2)}, u32[]{:S(2)}) collective-permute-start(bf16[288,880]{1,0:T(8,128)(2,1)S(1)} %slice.76), channel_id=1, source_target_pairs={{0,3},{1,0},{2,1},{3,2},{4,7},{5,4},{6,5},{7,6},{8,11},{9,8},{10,9... | collective-permute-start | bytes 1520648 | tf_op jit(solution)/shard_map/ppermute | solution.py:17
  69.6 2.6 %fusion.6 = f32[560,880]{1,0:T(8,128)S(1)} fusion(bf16[1680,2240]{1,0:T(8,128)(2,1)S(1)} %bitcast.59, s32[]{:T(128)S(6)} %select_n.116, bf16[560,880]{1,0:T(8,128)(2,1)S(1)} %bitcast.49, bf16[560,880]{1,0:T(8,128)(2,1)S(1)} %bitcast.45, bf16[560,880]{1,0:T(8,128)(2,1)S(1)} %bitcast.53), kind=kOutput, calls=%fused_computation.7 | convolution fusion | flops 1664678400 | bytes 7132164 | tf_op jit(solution)/shard_map/dot_general | solution.py:96
  72.1 0.0 copy-start.2
  72.1 0.0 collective-permute-done.16
  72.2 0.1 fusion.24
  72.3 3.5 %collective-permute-start.17 = (bf16[272,880]{1,0:T(8,128)(2,1)S(1)}, bf16[272,880]{1,0:T(8,128)(2,1)S(1)}, u32[]{:S(2)}, u32[]{:S(2)}) collective-permute-start(bf16[272,880]{1,0:T(8,128)(2,1)S(1)} %fusion.24), channel_id=1, source_target_pairs={{0,3},{1,0},{2,1},{3,2},{4,7},{5,4},{6,5},{7,6},{8,11},{9,8},{10,9... | collective-permute-start | bytes 1436168 | tf_op jit(solution)/shard_map/ppermute | solution.py:17
  75.8 0.4 collective-permute-done.12
  76.2 0.1 fusion.15
  76.3 0.1 collective-permute-start.13
  76.5 0.5 bitcast_multiply_fusion
  77.0 9.7 %collective-permute-done.15 = bf16[272,880]{1,0:T(8,128)(2,1)S(1)} collective-permute-done((bf16[272,880]{1,0:T(8,128)(2,1)S(1)}, bf16[272,880]{1,0:T(8,128)(2,1)S(1)}, u32[]{:S(2)}, u32[]{:S(2)}) %collective-permute-start.15) | collective-permute-done | bytes 478752 | tf_op jit(solution)/shard_map/ppermute | solution.py:17
  86.7 6.1 %collective-permute-done.17 = bf16[272,880]{1,0:T(8,128)(2,1)S(1)} collective-permute-done((bf16[272,880]{1,0:T(8,128)(2,1)S(1)}, bf16[272,880]{1,0:T(8,128)(2,1)S(1)}, u32[]{:S(2)}, u32[]{:S(2)}) %collective-permute-start.17) | collective-permute-done | bytes 478752 | tf_op jit(solution)/shard_map/ppermute | solution.py:17
  92.8 0.2 fusion.23
  93.0 0.0 collective-permute-done.14
  93.0 3.7 %collective-permute-done.13 = bf16[288,880]{1,0:T(8,128)(2,1)S(1)} collective-permute-done((bf16[288,880]{1,0:T(8,128)(2,1)S(1)}, bf16[288,880]{1,0:T(8,128)(2,1)S(1)}, u32[]{:S(2)}, u32[]{:S(2)}) %collective-permute-start.13) | collective-permute-done | bytes 506912 | tf_op jit(solution)/shard_map/ppermute | solution.py:17
  96.8 0.3 fusion.14
  97.0 1.0 %maximum_bitcast_fusion = bf16[880,560]{0,1:T(8,128)(2,1)} fusion(bf16[272,880]{1,0:T(8,128)(2,1)S(1)} %fusion.23, bf16[288,880]{1,0:T(8,128)(2,1)S(1)} %fusion.14), kind=kLoop, calls=%fused_computation.28 | loop fusion | flops 1971200 | bytes 1971200 | tf_op jit(solution)/shard_map/transpose | solution.py:113
  (15 shorter events, 0.2 us)
Async XLA Ops:
  0.0 1.5 %copy-start = (bf16[880,560]{0,1:T(8,128)(2,1)S(1)}, bf16[880,560]{0,1:T(8,128)(2,1)}, u32[]{:S(2)}) copy-start(bf16[880,560]{0,1:T(8,128)(2,1)} %param.7) | copy-start | bytes 2956804
  1.5 34.8 %copy-start.1 = (bf16[880,560]{0,1:T(8,128)(2,1)S(1)}, bf16[880,560]{0,1:T(8,128)(2,1)}, u32[]{:S(2)}) copy-start(bf16[880,560]{0,1:T(8,128)(2,1)} %param.5) | copy-start | bytes 2956804
  2.7 4.2 %collective-permute-start = (bf16[280,112]{1,0:T(8,128)(2,1)S(1)}, bf16[280,112]{1,0:T(8,128)(2,1)S(1)}, u32[]{:S(2)}, u32[]{:S(2)}) collective-permute-start(bf16[280,112]{1,0:T(8,128)(2,1)S(1)} %dynamic-slice_convert_fusion), channel_id=1, source_target_pairs={{0,4},{4,0},{1,5},{5,1},{2,6},{6,2},{3,7},{7,3},{8,12},{12,8},{9,1... | collective-permute-start | bytes 188168 | tf_op jit(solution)/shard_map/ppermute | solution.py:17
  6.9 3.3 %collective-permute-start.3 = (bf16[280,112]{1,0:T(8,128)(2,1)S(1)}, bf16[280,112]{1,0:T(8,128)(2,1)S(1)}, u32[]{:S(2)}, u32[]{:S(2)}) collective-permute-start(bf16[280,112]{1,0:T(8,128)(2,1)S(1)} %fusion.44), channel_id=1, source_target_pairs={{0,24},{8,0},{16,8},{24,16},{1,25},{9,1},{17,9},{25,17},{2,26},{10... | collective-permute-start | bytes 188168 | tf_op jit(solution)/shard_map/ppermute | solution.py:17
  7.7 4.7 %collective-permute-start.2 = (bf16[280,112]{1,0:T(8,128)(2,1)S(1)}, bf16[280,112]{1,0:T(8,128)(2,1)S(1)}, u32[]{:S(2)}, u32[]{:S(2)}) collective-permute-start(bf16[280,112]{1,0:T(8,128)(2,1)S(1)} %fusion.44), channel_id=1, source_target_pairs={{0,16},{8,24},{16,0},{24,8},{1,17},{9,25},{17,1},{25,9},{2,18},{10... | collective-permute-start | bytes 188168 | tf_op jit(solution)/shard_map/ppermute | solution.py:17
  8.3 6.3 %collective-permute-start.1 = (bf16[280,112]{1,0:T(8,128)(2,1)S(1)}, bf16[280,112]{1,0:T(8,128)(2,1)S(1)}, u32[]{:S(2)}, u32[]{:S(2)}) collective-permute-start(bf16[280,112]{1,0:T(8,128)(2,1)S(1)} %fusion.44), channel_id=1, source_target_pairs={{0,8},{8,16},{16,24},{24,0},{1,9},{9,17},{17,25},{25,1},{2,10},{10... | collective-permute-start | bytes 188168 | tf_op jit(solution)/shard_map/ppermute | solution.py:17
  14.6 6.9 %collective-permute-start.5 = (bf16[280,112]{1,0:T(8,128)(2,1)S(1)}, bf16[280,112]{1,0:T(8,128)(2,1)S(1)}, u32[]{:S(2)}, u32[]{:S(2)}) collective-permute-start(bf16[280,112]{1,0:T(8,128)(2,1)S(1)} %get-tuple-element.9), channel_id=1, source_target_pairs={{0,224},{32,0},{64,32},{96,64},{128,96},{160,128},{192,160},{224,1... | collective-permute-start | bytes 188168 | tf_op jit(solution)/shard_map/ppermute | solution.py:17
  20.1 4.4 %collective-permute-start.4 = (bf16[280,112]{1,0:T(8,128)(2,1)S(1)}, bf16[280,112]{1,0:T(8,128)(2,1)S(1)}, u32[]{:S(2)}, u32[]{:S(2)}) collective-permute-start(bf16[280,112]{1,0:T(8,128)(2,1)S(1)} %get-tuple-element.9), channel_id=1, source_target_pairs={{0,32},{32,64},{64,96},{96,128},{128,160},{160,192},{192,224},{224... | collective-permute-start | bytes 188168 | tf_op jit(solution)/shard_map/ppermute | solution.py:17
  24.6 7.4 %collective-permute-start.6 = (bf16[280,112]{1,0:T(8,128)(2,1)S(1)}, bf16[280,112]{1,0:T(8,128)(2,1)S(1)}, u32[]{:S(2)}, u32[]{:S(2)}) collective-permute-start(bf16[280,112]{1,0:T(8,128)(2,1)S(1)} %get-tuple-element.13), channel_id=1, source_target_pairs={{0,96},{32,128},{64,160},{96,192},{128,224},{160,0},{192,32},{224,... | collective-permute-start | bytes 188168 | tf_op jit(solution)/shard_map/ppermute | solution.py:17
  24.7 7.3 %collective-permute-start.7 = (bf16[280,112]{1,0:T(8,128)(2,1)S(1)}, bf16[280,112]{1,0:T(8,128)(2,1)S(1)}, u32[]{:S(2)}, u32[]{:S(2)}) collective-permute-start(bf16[280,112]{1,0:T(8,128)(2,1)S(1)} %get-tuple-element.14), channel_id=1, source_target_pairs={{0,160},{32,192},{64,224},{96,0},{128,32},{160,64},{192,96},{224,1... | collective-permute-start | bytes 188168 | tf_op jit(solution)/shard_map/ppermute | solution.py:17
  32.7 5.4 %collective-permute-start.8 = (bf16[280,112]{1,0:T(8,128)(2,1)}, bf16[280,112]{1,0:T(8,128)(2,1)}, u32[]{:S(2)}, u32[]{:S(2)}) collective-permute-start(bf16[280,112]{1,0:T(8,128)(2,1)} %get-tuple-element.7), channel_id=1, source_target_pairs={{0,4},{4,0},{1,5},{5,1},{2,6},{6,2},{3,7},{7,3},{8,12},{12,8},{9,1... | collective-permute-start | bytes 188168 | tf_op jit(solution)/shard_map/ppermute | solution.py:17
  36.3 15.6 %collective-permute-start.11 = (bf16[5,112,880]{2,1,0:T(8,128)(2,1)S(1)}, bf16[5,112,880]{2,1,0:T(8,128)(2,1)}, u32[]{:S(2)}, u32[]{:S(2)}) collective-permute-start(bf16[5,112,880]{2,1,0:T(8,128)(2,1)S(1)} %bitcast.39), channel_id=1, source_target_pairs={{0,252},{4,0},{8,4},{12,8},{16,12},{20,16},{24,20},{28,24},{32,28}... | collective-permute-start | bytes 2956808 | tf_op jit(solution)/shard_map/ppermute | solution.py:17
  36.4 17.4 %collective-permute-start.9 = (bf16[5,112,880]{2,1,0:T(8,128)(2,1)S(1)}, bf16[5,112,880]{2,1,0:T(8,128)(2,1)S(1)}, u32[]{:S(2)}, u32[]{:S(2)}) collective-permute-start(bf16[5,112,880]{2,1,0:T(8,128)(2,1)S(1)} %bitcast.40), channel_id=1, source_target_pairs={{0,4},{4,8},{8,12},{12,16},{16,20},{20,24},{24,28},{28,32},{32,36}... | collective-permute-start | bytes 2956808 | tf_op jit(solution)/shard_map/ppermute | solution.py:17
  38.1 13.8 %collective-permute-start.10 = (bf16[5,112,112]{2,1,0:T(8,128)(2,1)}, bf16[5,112,112]{2,1,0:T(8,128)(2,1)}, u32[]{:S(2)}, u32[]{:S(2)}) collective-permute-start(bf16[5,112,112]{2,1,0:T(8,128)(2,1)} %get-tuple-element.15), channel_id=1, source_target_pairs={{0,252},{4,0},{8,4},{12,8},{16,12},{20,16},{24,20},{28,24},{32,28}... | collective-permute-start | bytes 376328 | tf_op jit(solution)/shard_map/ppermute | solution.py:17
  39.6 15.0 %slice-start = ((s8[7741440]{0:T(1024)(128)(4,1)}), s8[4194304]{0:T(1024)(128)(4,1)S(1)}, s32[]{:S(2)}) async-start(s8[7741440]{0:T(1024)(128)(4,1)} %bitcast.54), calls=%async_computation | async-start | bytes 8388608
  53.8 2.0 %slice-start.1 = ((s8[7741440]{0:T(1024)(128)(4,1)}), s8[3547136]{0:T(1024)(128)(4,1)S(1)}, s32[]{:S(2)}) async-start(s8[7741440]{0:T(1024)(128)(4,1)} %bitcast.54), calls=%async_computation.1 | async-start | bytes 7094272
  58.4 13.8 %collective-permute-start.16 = (bf16[272,880]{1,0:T(8,128)(2,1)S(1)}, bf16[272,880]{1,0:T(8,128)(2,1)S(1)}, u32[]{:S(2)}, u32[]{:S(2)}) collective-permute-start(bf16[272,880]{1,0:T(8,128)(2,1)S(1)} %slice.50), channel_id=1, source_target_pairs={{0,3},{1,0},{2,1},{3,2},{4,7},{5,4},{6,5},{7,6},{8,11},{9,8},{10,9... | collective-permute-start | bytes 1436168 | tf_op jit(solution)/shard_map/ppermute | solution.py:17
  61.2 15.0 %collective-permute-start.12 = (bf16[288,880]{1,0:T(8,128)(2,1)S(1)}, bf16[288,880]{1,0:T(8,128)(2,1)S(1)}, u32[]{:S(2)}, u32[]{:S(2)}) collective-permute-start(bf16[288,880]{1,0:T(8,128)(2,1)S(1)} %slice.44), channel_id=1, source_target_pairs={{0,1},{1,2},{2,3},{3,0},{4,5},{5,6},{6,7},{7,4},{8,9},{9,10},{10,1... | collective-permute-start | bytes 1520648 | tf_op jit(solution)/shard_map/ppermute | solution.py:17
  63.9 22.8 %collective-permute-start.15 = (bf16[272,880]{1,0:T(8,128)(2,1)S(1)}, bf16[272,880]{1,0:T(8,128)(2,1)S(1)}, u32[]{:S(2)}, u32[]{:S(2)}) collective-permute-start(bf16[272,880]{1,0:T(8,128)(2,1)S(1)} %slice.77), channel_id=1, source_target_pairs={{0,1},{1,2},{2,3},{3,0},{4,5},{5,6},{6,7},{7,4},{8,9},{9,10},{10,1... | collective-permute-start | bytes 1436168 | tf_op jit(solution)/shard_map/ppermute | solution.py:17
  66.6 26.4 %collective-permute-start.14 = (bf16[288,880]{1,0:T(8,128)(2,1)S(1)}, bf16[288,880]{1,0:T(8,128)(2,1)S(1)}, u32[]{:S(2)}, u32[]{:S(2)}) collective-permute-start(bf16[288,880]{1,0:T(8,128)(2,1)S(1)} %slice.76), channel_id=1, source_target_pairs={{0,3},{1,0},{2,1},{3,2},{4,7},{5,4},{6,5},{7,6},{8,11},{9,8},{10,9... | collective-permute-start | bytes 1520648 | tf_op jit(solution)/shard_map/ppermute | solution.py:17
  72.1 4.3 %copy-start.2 = (bf16[880,560]{0,1:T(8,128)(2,1)S(1)}, bf16[880,560]{0,1:T(8,128)(2,1)}, u32[]{:S(2)}) copy-start(bf16[880,560]{0,1:T(8,128)(2,1)} %param.9) | copy-start | bytes 2956804
  72.3 20.4 %collective-permute-start.17 = (bf16[272,880]{1,0:T(8,128)(2,1)S(1)}, bf16[272,880]{1,0:T(8,128)(2,1)S(1)}, u32[]{:S(2)}, u32[]{:S(2)}) collective-permute-start(bf16[272,880]{1,0:T(8,128)(2,1)S(1)} %fusion.24), channel_id=1, source_target_pairs={{0,3},{1,0},{2,1},{3,2},{4,7},{5,4},{6,5},{7,6},{8,11},{9,8},{10,9... | collective-permute-start | bytes 1436168 | tf_op jit(solution)/shard_map/ppermute | solution.py:17
  76.3 20.4 %collective-permute-start.13 = (bf16[288,880]{1,0:T(8,128)(2,1)S(1)}, bf16[288,880]{1,0:T(8,128)(2,1)S(1)}, u32[]{:S(2)}, u32[]{:S(2)}) collective-permute-start(bf16[288,880]{1,0:T(8,128)(2,1)S(1)} %fusion.15), channel_id=1, source_target_pairs={{0,1},{1,2},{2,3},{3,0},{4,5},{5,6},{6,7},{7,4},{8,9},{9,10},{10,1... | collective-permute-start | bytes 1520648 | tf_op jit(solution)/shard_map/ppermute | solution.py:17
